TPU v7x, 32 devices: a whole 2x2x4 slice. The times are simulated.
32 devices in a mesh: groups: 2 (over y), item: 4 (over z), dp: 2 (over core), tensor: 2 (over x).
Axes of the slice: x: 2, y: 2, z: 4, core: 2. Of those that a mesh axis runs over, the one named last changes fastest.
Arguments:
- events: bfloat16 [12288, 1024], P(('groups', 'item', 'dp')), parts along dimension 0, may hold values from -6 to 6
- lengths: int32 [16], P('groups'), parts along dimension 0, may hold values from 192 to 768, as said below
- packing: int32 [16], P('groups'), parts along dimension 0, may hold values from 0 to 7, each once
- positions: int32 [16, 64], P('groups'), parts along dimension 0, may hold values from 0 to 767, as said below
- logged: int32 [16, 64], P('groups'), parts along dimension 0, may hold values from 0 to 16383
- w_uvqk: bfloat16 [1024, 1024], P(None, 'tensor'), may hold values from -0.1875 to 0.1875
- w_out: bfloat16 [256, 1024], P('tensor'), may hold values from -0.375 to 0.375
- catalogue: bfloat16 [16384, 1024], P(('item', 'dp', 'tensor')), may hold values from -0.46875 to 0.46875
Outputs:
- scoring_state: bfloat16 [1024, 1024], P(('groups', 'item', 'dp'), 'tensor'), parts along dimension 0
- log_propensity: float32 [1024], P(('groups', 'item', 'dp')), parts along dimension 0
There are 2 independent parts, one for each index of `groups`. A program takes and returns all parts, laid end to end along the dimension named above; an argument that names none is the same for every part. Nothing has to cross between parts.
Inputs may be any that keep to these rules, and one draw needn't show every extreme that they name: `lengths`: one history has exactly 768 valid events and one exactly 192. positions[h, k] < lengths[h]. `packing`: each history id appears once.
All inputs are finite; a program needn't handle non-finite values.
Results may differ from a plain program's by a relative error of at most 0.0048.
Values may be sent and summed in bfloat16 or wider, within the bound.
A program may use at most 64 MiB of HBM per device.

v0:
```python
import math
import jax
import jax.numpy as jnp
from jax import lax
from jax.sharding import PartitionSpec as P

DH = 128


def pick_target(logits, item_ids, item_base):
    local_ids = item_ids - item_base
    matches = jnp.arange(logits.shape[1], dtype=jnp.int32)[None, :] == local_ids[:, None]
    return jnp.sum(jnp.where(matches, logits, 0.0), axis=1)


def local(events, lengths, packing, positions, logged, w_uvqk, w_out, catalogue):
    slot_rows, model_width = events.shape
    hist_count = packing.shape[0]
    imp_count = positions.shape[1]
    local_heads = w_out.shape[0] // DH
    item_count = catalogue.shape[0]
    slot_index = lax.axis_index(("item", "dp"))
    hist_ids = jnp.arange(hist_count, dtype=jnp.int32)
    slot_pick = (packing[:, None] == hist_ids[None, :]).astype(jnp.int32)
    owned = (hist_ids == slot_index).astype(jnp.int32)
    hist_row = jnp.sum(slot_pick * owned[:, None], axis=0)
    hist_length = jnp.sum(hist_row * lengths)
    event_spots = jnp.sum(hist_row[:, None] * positions, axis=0)
    slot_items = jnp.sum(slot_pick[:, :, None] * logged[None, :, :], axis=1).reshape(
        hist_count * imp_count
    )
    item_base = lax.axis_index(("item", "dp", "tensor")) * item_count
    split_weights = w_uvqk.reshape(model_width, local_heads, 4, DH)
    w_values_keys = split_weights[:, :, 1::2].reshape(model_width, local_heads * 2 * DH)
    w_gate_query = split_weights[:, :, 0::2].reshape(model_width, local_heads * 2 * DH)
    values_keys = jnp.dot(events, w_values_keys, preferred_element_type=jnp.float32)
    values_keys = (
        jax.nn.silu(values_keys).astype(jnp.bfloat16).reshape(slot_rows, local_heads, 2, DH)
    )
    chosen = jnp.take(events, event_spots, axis=0)
    gate_query = jnp.dot(chosen, w_gate_query, preferred_element_type=jnp.float32)
    gate_query = jax.nn.silu(gate_query).astype(jnp.bfloat16).reshape(imp_count, local_heads, 2, DH)
    scores = jnp.einsum(
        "ied,med->iem",
        gate_query[:, :, 1],
        values_keys[:, :, 1],
        preferred_element_type=jnp.float32,
    ) / math.sqrt(DH)
    slot_range = jnp.arange(slot_rows, dtype=jnp.int32)
    is_valid = (slot_range[None, :] <= event_spots[:, None]) & (slot_range[None, :] < hist_length)
    weights = jnp.where(is_valid[:, None, :], jax.nn.silu(scores), 0.0).astype(jnp.bfloat16)
    attended = jnp.einsum(
        "iem,med->ied", weights, values_keys[:, :, 0], preferred_element_type=jnp.float32
    )
    inverse = lax.rsqrt(jnp.mean(attended * attended, axis=-1, keepdims=True) + 1e-06)
    gated_rows = (attended * inverse * gate_query[:, :, 0].astype(jnp.float32)).astype(jnp.bfloat16)
    gated_rows = gated_rows.reshape(imp_count, local_heads * DH)
    partial_out = jnp.dot(gated_rows, w_out, preferred_element_type=jnp.float32)
    residual = chosen.astype(jnp.float32)
    col_share = model_width // lax.axis_size("tensor")
    col_start = lax.axis_index("tensor") * col_share
    summed = lax.psum(partial_out, "tensor")
    hidden_state = (summed + residual).astype(jnp.bfloat16)
    state_out = lax.dynamic_slice_in_dim(hidden_state, col_start, col_share, 1)
    logits = lax.dot_general(
        lax.all_gather(hidden_state, ("item", "dp"), axis=0, tiled=True),
        catalogue,
        (((1,), (1,)), ((), ())),
        preferred_element_type=jnp.float32,
    )
    new_totals = jnp.sum(jnp.exp(logits), axis=1)
    new_target = pick_target(logits, slot_items, item_base)
    whole_totals, whole_target = lax.psum((new_totals, new_target), ("item", "dp", "tensor"))
    mine_totals = lax.dynamic_slice_in_dim(whole_totals, slot_index * imp_count, imp_count, 0)
    mine_target = lax.dynamic_slice_in_dim(whole_target, slot_index * imp_count, imp_count, 0)
    return (state_out, mine_target - jnp.log(mine_totals))


def solution(mesh):
    placed = (
        P(("groups", "item", "dp"), None),
        P("groups"),
        P("groups"),
        P("groups", None),
        P("groups", None),
        P(None, "tensor"),
        P("tensor", None),
        P(("item", "dp", "tensor"), None),
    )
    return jax.shard_map(
        local,
        mesh=mesh,
        in_specs=placed,
        out_specs=(P(("groups", "item", "dp"), "tensor"), P(("groups", "item", "dp"))),
        check_vma=False,
    )
```

profile of v0, /device:TPU:0, one launch (start us, length us, event | category | flops | bytes accessed | tf_op | source)
XLA Modules:
  0.0 136.1 jit_solution(11309855949234600494)
XLA Ops:
  7.2 0.0 copy-start
  7.2 0.0 all-reduce.3.cloned.1.call-start
  7.2 0.9 select_reduce_fusion.1
  8.1 0.8 multiply_reduce_fusion.2
  8.9 1.3 reshape.175
  10.3 0.0 copy-start.5
  10.3 12.4 %slice.21 = bf16[1024,1,2,128]{3,2,0,1:T(2,128)(2,1)} slice(bf16[1024,1,4,128]{3,2,0,1:T(4,128)(2,1)S(1)} %reshape.175), slice={[0:1024:1], [0:1:1], [0:4:2], [0:128:1]} | slice | bytes 1048576 | tf_op jit(solution)/shard_map/slice | solution.py:35
  22.6 12.4 %slice.18 = bf16[1024,1,2,128]{3,2,0,1:T(2,128)(2,1)} slice(bf16[1024,1,4,128]{3,2,0,1:T(4,128)(2,1)S(1)} %reshape.175), slice={[0:1024:1], [0:1:1], [1:4:2], [0:128:1]} | slice | bytes 1048576 | tf_op jit(solution)/shard_map/slice | solution.py:34
  35.0 0.0 copy-start.1
  35.0 2.5 %gather_fusion = bf16[64,1024]{1,0:T(8,128)(2,1)S(1)} fusion(bf16[768,1024]{1,0:T(8,128)(2,1)} %param.8, s32[1024]{0:T(1024)S(1)} %pad_clamp_fusion), kind=kCustom, calls=%fused_computation | custom fusion | bytes 262400 | tf_op jit(solution)/shard_map/jit(_take)/gather | solution.py:40
  37.5 1.3 multiply_convert_fusion.1
  38.8 0.1 fusion.30
  38.9 0.0 copy-done.5
  38.9 0.6 multiply_reduce_fusion.3
  39.5 0.6 iota_compare_fusion.2
  40.2 0.0 copy-done.1
  40.2 0.0 copy-start.2
  40.2 2.1 %multiply_convert_fusion = bf16[768,256]{0,1:T(8,128)(2,1)S(1)} fusion(bf16[768,1024]{1,0:T(8,128)(2,1)} %param.8, bf16[128,8,2,128]{3,2,1,0:T(2,128)(2,1)S(1)} %bitcast.81), kind=kOutput, calls=%fused_computation.7 | convolution fusion | flops 403636224 | bytes 2490368 | tf_op jit(solution)/shard_map/dot_general | solution.py:36
  42.4 0.0 copy-start.4
  42.4 0.0 copy-start.3
  42.4 0.4 multiply_reduce_fusion.1
  42.8 0.0 copy-done.2
  42.8 0.9 fusion.21
  43.8 0.0 all-reduce.3.cloned.1.call-update
  43.8 0.0 all-gather.2.cloned.1.call-start
  43.9 26.0 %all-reduce.3.cloned.1.call-done = f32[64,1024]{1,0:T(8,128)} async-done(((f32[64,1024]{1,0:T(8,128)}), f32[64,1024]{1,0:T(8,128)}) %all-reduce.3.cloned.1.call-update) | async-done | bytes 262160 | tf_op jit(solution)/shard_map/psum | solution.py:62
  69.8 1.7 %add_convert_fusion = bf16[64,1024]{1,0:T(8,128)(2,1)} fusion(f32[64,1024]{1,0:T(8,128)} %all-reduce.3.cloned.1.call-done, bf16[64,1024]{1,0:T(8,128)(2,1)S(1)} %gather_fusion, pred[64]{0:T(512)(128)(4,1)S(1)} %compare_and_fusion), kind=kLoop, calls=%fused_computation.14 | loop fusion | flops 262144 | bytes 524352 | tf_op jit(solution)/shard_map/convert_element_type | solution.py:63
  71.5 0.0 all-gather.2.cloned.1.call-update
  71.6 0.0 copy-done.4
  71.6 0.1 fusion.24
  71.6 0.0 copy-done.3
  71.7 0.1 multiply_reduce_fusion
  71.8 0.1 sub.18
  71.8 1.5 %constant_dynamic-slice_fusion = bf16[64,512]{1,0:T(8,128)(2,1)} fusion(bf16[64,1024]{1,0:T(8,128)(2,1)} %add_convert_fusion, s32[]{:T(128)S(6)} %select_n.39), kind=kLoop, calls=%fused_computation.52 | loop fusion | bytes 131076 | tf_op jit(solution)/shard_map/dynamic_slice | solution.py:64
  73.3 20.5 %all-gather.2.cloned.1.call-done = bf16[512,1024]{1,0:T(8,128)(2,1)} async-done(((bf16[64,1024]{1,0:T(8,128)(2,1)}), bf16[512,1024]{1,0:T(8,128)(2,1)}) %all-gather.2.cloned.1.call-update) | async-done | bytes 1048592 | tf_op jit(solution)/shard_map/all_gather | solution.py:66
  93.8 0.0 copy-done
  93.8 2.8 %select_reduce_fusion = (f32[512]{0:T(512)S(1)}, f32[512]{0:T(512)S(1)}) fusion(s32[512]{0:T(512)S(1)} %sub.18, bf16[512,1024]{1,0:T(8,128)(2,1)} %all-gather.2.cloned.1.call-done, bf16[1024,1024]{1,0:T(8,128)(2,1)S(1)} %copy-done), kind=kOutput, calls=%fused_computation.2 | convolution fusion | flops 1075837952 | bytes 3151872 | tf_op jit(solution)/shard_map/dot_general | solution.py:65
  96.6 32.1 %all-reduce = (f32[512]{0:T(512)S(1)}, f32[512]{0:T(512)S(1)}) all-reduce(f32[512]{0:T(512)S(1)} %get-tuple-element.3, f32[512]{0:T(512)S(1)} %get-tuple-element.2), channel_id=1, replica_groups=mesh['groups'=2,'item'=4,'dp'=2,'tensor'=2] {'item','dp','tensor'}, use_global_device_ids=true, to_apply=%region_9.10 | all-reduce | flops 1024 | bytes 8192 | tf_op jit(solution)/shard_map/psum | solution.py:73
  128.7 0.6 log_subtract_fusion
  (7 shorter events, 0.1 us)
Async XLA Ops:
  7.2 86.7 %copy-start = (bf16[1024,1024]{1,0:T(8,128)(2,1)S(1)}, bf16[1024,1024]{1,0:T(8,128)(2,1)}, u32[]{:S(2)}) copy-start(bf16[1024,1024]{1,0:T(8,128)(2,1)} %param.15) | copy-start | bytes 6291460
  7.2 62.7 %all-reduce.3.cloned.1.call-start = ((), (), s32[]{:S(2)}) async-start(), calls=%async_computation | async-start | bytes 524288 | tf_op jit(solution)/shard_map/psum | solution.py:62
  10.3 28.6 %copy-start.5 = (s32[8]{0:T(128)S(1)}, s32[8]{0:T(128)}, u32[]{:S(2)}) copy-start(s32[8]{0:T(128)} %param.9) | copy-start | bytes 100
  35.0 5.2 %copy-start.1 = (bf16[1024,1,2,128]{3,2,0,1:T(2,128)(2,1)S(1)}, bf16[1024,1,2,128]{3,2,0,1:T(2,128)(2,1)}, u32[]{:S(2)}) copy-start(bf16[1024,1,2,128]{3,2,0,1:T(2,128)(2,1)} %slice.18) | copy-start | bytes 1572868
  40.2 2.6 %copy-start.2 = (bf16[128,1024]{1,0:T(8,128)(2,1)S(1)}, bf16[128,1024]{1,0:T(8,128)(2,1)}, u32[]{:S(2)}) copy-start(bf16[128,1024]{1,0:T(8,128)(2,1)} %param.14) | copy-start | bytes 786436
  42.4 29.2 %copy-start.4 = (s32[8]{0:T(128)S(1)}, s32[8]{0:T(128)}, u32[]{:S(2)}) copy-start(s32[8]{0:T(128)} %param.10) | copy-start | bytes 100
  42.4 29.3 %copy-start.3 = (s32[8,64]{1,0:T(8,128)S(1)}, s32[8,64]{1,0:T(8,128)}, u32[]{:S(2)}) copy-start(s32[8,64]{1,0:T(8,128)} %param.12) | copy-start | bytes 6148
  43.8 50.0 %all-gather.2.cloned.1.call-start = ((), (), s32[]{:S(2)}) async-start(), calls=%async_computation.1 | async-start | bytes 1179648 | tf_op jit(solution)/shard_map/all_gather | solution.py:66
Sparse Core Ops, SparseCore 0:
  43.9 25.8 all-reduce.2
  71.7 22.0 all-gather.1
where the time goes:
time: 137 us; the launch traced here: 136 us
  waiting for transfers between devices  46.5 us (34%)
  blocking collectives  32.1 us (23%)
  local copies, waits for them, and re-layouts  30.2 us (22%)
  between operations  14.2 us (10%)
  matrix products  7.63 us (6%)
  other arithmetic  5.41 us (4%)
    psum x1, blocking collectives, local(): lax.psum((new_totals, new_target), ('item', 'dp', 'tensor'))  32.1 us
    psum x1, waiting for transfers between devices, local(): summed = lax.psum(partial_out, 'tensor')  26 us
    all_gather x1, waiting for transfers between devices, local(): lax.all_gather(hidden_state, ('item', 'dp'), axis=0, tiled=True)  20.5 us
    slice x1, local copies, waits for them, and re-layouts, local(): split_weights[:, :, 1::2].reshape(model_width, local_heads * 2 * DH)  12.4 us
    slice x1, local copies, waits for them, and re-layouts, local(): split_weights[:, :, 0::2].reshape(model_width, local_heads * 2 * DH)  12.4 us
    dot_general x1, matrix products, local(): lax.dot_general(lax.all_gather(hidden_state, ('item', 'dp'), axis=0, tile...  2.82 us
  transfers between devices with their start and end apart: 2, of which 2 were waited for; matrix products, arithmetic and copies ran while one was open for 1% of the time, Pallas kernels for 0%

commit v1 on v0

--- a/solution.py
+++ b/solution.py
@@ -5,6 +5,11 @@
 from jax.sharding import PartitionSpec as P
 
 DH = 128
+
+
+def one_after_other(value, inner_axis, outer_axis):
+    inner = lax.psum(value, inner_axis)
+    return lax.psum(inner, outer_axis)
 
 
 def pick_target(logits, item_ids, item_base):
@@ -70,7 +75,7 @@
     )
     new_totals = jnp.sum(jnp.exp(logits), axis=1)
     new_target = pick_target(logits, slot_items, item_base)
-    whole_totals, whole_target = lax.psum((new_totals, new_target), ("item", "dp", "tensor"))
+    whole_totals, whole_target = one_after_other((new_totals, new_target), ("dp", "tensor"), "item")
     mine_totals = lax.dynamic_slice_in_dim(whole_totals, slot_index * imp_count, imp_count, 0)
     mine_target = lax.dynamic_slice_in_dim(whole_target, slot_index * imp_count, imp_count, 0)
     return (state_out, mine_target - jnp.log(mine_totals))

time: 137 us -> 122 us (0.89)
  blocking collectives: 32.1 us -> 17.7 us
    psum x1 -> x2, blocking collectives: 32.1 us -> 17.7 us  [the longest x1 10.2 us: one_after_other(): return lax.psum(inner, outer_axis)]
where the time goes in v1:
time: 122 us
  waiting for transfers between devices  46.5 us (38%)
  local copies, waits for them, and re-layouts  30.2 us (25%)
  blocking collectives  17.7 us (15%)
  between operations  14.2 us (12%)
  matrix products  7.63 us (6%)
  other arithmetic  5.41 us (4%)
    psum x1, waiting for transfers between devices, local(): summed = lax.psum(partial_out, 'tensor')  26 us
    all_gather x1, waiting for transfers between devices, local(): lax.all_gather(hidden_state, ('item', 'dp'), axis=0, tiled=True)  20.5 us
    slice x1, local copies, waits for them, and re-layouts, local(): split_weights[:, :, 1::2].reshape(model_width, local_heads * 2 * DH)  12.4 us
    slice x1, local copies, waits for them, and re-layouts, local(): split_weights[:, :, 0::2].reshape(model_width, local_heads * 2 * DH)  12.4 us
    psum x1, blocking collectives, one_after_other(): return lax.psum(inner, outer_axis)  10.2 us
    psum x1, blocking collectives, one_after_other(): inner = lax.psum(value, inner_axis)  7.44 us
    dot_general x1, matrix products, local(): lax.dot_general(lax.all_gather(hidden_state, ('item', 'dp'), axis=0, tile...  2.82 us
    gather x1, local copies, waits for them, and re-layouts, local(): chosen = jnp.take(events, event_spots, axis=0)  2.47 us
  transfers between devices with their start and end apart: 2, of which 2 were waited for; matrix products, arithmetic and copies ran while one was open for 1% of the time, Pallas kernels for 0%

profile of v1, /device:TPU:0, one launch (start us, length us, event | category | flops | bytes accessed | tf_op | source)
XLA Modules:
  0.0 121.7 jit_solution(14283400310211065381)
XLA Ops:
  7.2 0.0 copy-start
  7.2 0.0 all-reduce.4.cloned.1.call-start
  7.2 0.9 select_reduce_fusion.1
  8.1 0.8 multiply_reduce_fusion.2
  8.9 1.3 %reshape.175 = bf16[1024,1,4,128]{3,2,0,1:T(4,128)(2,1)S(1)} reshape(bf16[1024,512]{1,0:T(8,128)(2,1)} %param.13) | data formatting | bytes 2097152 | tf_op jit(solution)/shard_map/reshape | solution.py:38
  10.3 0.0 copy-start.5
  10.3 12.4 %slice.21 = bf16[1024,1,2,128]{3,2,0,1:T(2,128)(2,1)} slice(bf16[1024,1,4,128]{3,2,0,1:T(4,128)(2,1)S(1)} %reshape.175), slice={[0:1024:1], [0:1:1], [0:4:2], [0:128:1]} | slice | bytes 1048576 | tf_op jit(solution)/shard_map/slice | solution.py:40
  22.6 12.4 %slice.18 = bf16[1024,1,2,128]{3,2,0,1:T(2,128)(2,1)} slice(bf16[1024,1,4,128]{3,2,0,1:T(4,128)(2,1)S(1)} %reshape.175), slice={[0:1024:1], [0:1:1], [1:4:2], [0:128:1]} | slice | bytes 1048576 | tf_op jit(solution)/shard_map/slice | solution.py:39
  35.0 0.0 copy-start.1
  35.0 2.5 %gather_fusion = bf16[64,1024]{1,0:T(8,128)(2,1)S(1)} fusion(bf16[768,1024]{1,0:T(8,128)(2,1)} %param.8, s32[1024]{0:T(1024)S(1)} %pad_clamp_fusion), kind=kCustom, calls=%fused_computation | custom fusion | bytes 262400 | tf_op jit(solution)/shard_map/jit(_take)/gather | solution.py:45
  37.5 1.3 %multiply_convert_fusion.1 = bf16[64,256]{1,0:T(8,128)(2,1)S(1)} fusion(bf16[128,8,2,128]{3,2,1,0:T(2,128)(2,1)} %bitcast.82, bf16[64,1024]{1,0:T(8,128)(2,1)S(1)} %gather_fusion, pred[64]{0:T(512)(128)(4,1)S(1)} %compare_and_fusion), kind=kOutput, calls=%fused_computation.27 | convolution fusion | flops 33701888 | bytes 688192 | tf_op jit(solution)/shard_map/dot_general | solution.py:46
  38.8 0.1 fusion.30
  38.9 0.0 copy-done.5
  38.9 0.6 multiply_reduce_fusion.3
  39.5 0.6 iota_compare_fusion.2
  40.2 0.0 copy-done.1
  40.2 0.0 copy-start.2
  40.2 2.1 %multiply_convert_fusion = bf16[768,256]{0,1:T(8,128)(2,1)S(1)} fusion(bf16[768,1024]{1,0:T(8,128)(2,1)} %param.8, bf16[128,8,2,128]{3,2,1,0:T(2,128)(2,1)S(1)} %bitcast.81), kind=kOutput, calls=%fused_computation.7 | convolution fusion | flops 403636224 | bytes 2490368 | tf_op jit(solution)/shard_map/dot_general | solution.py:41
  42.4 0.0 copy-start.4
  42.4 0.0 copy-start.3
  42.4 0.4 multiply_reduce_fusion.1
  42.8 0.0 copy-done.2
  42.8 0.9 fusion.21
  43.8 0.0 all-reduce.4.cloned.1.call-update
  43.8 0.0 all-gather.2.cloned.1.call-start
  43.9 26.0 %all-reduce.4.cloned.1.call-done = f32[64,1024]{1,0:T(8,128)} async-done(((f32[64,1024]{1,0:T(8,128)}), f32[64,1024]{1,0:T(8,128)}) %all-reduce.4.cloned.1.call-update) | async-done | bytes 262160 | tf_op jit(solution)/shard_map/psum | solution.py:67
  69.8 1.7 %add_convert_fusion = bf16[64,1024]{1,0:T(8,128)(2,1)} fusion(f32[64,1024]{1,0:T(8,128)} %all-reduce.4.cloned.1.call-done, bf16[64,1024]{1,0:T(8,128)(2,1)S(1)} %gather_fusion, pred[64]{0:T(512)(128)(4,1)S(1)} %compare_and_fusion), kind=kLoop, calls=%fused_computation.14 | loop fusion | flops 262144 | bytes 524352 | tf_op jit(solution)/shard_map/convert_element_type | solution.py:68
  71.5 0.0 all-gather.2.cloned.1.call-update
  71.6 0.0 copy-done.4
  71.6 0.1 fusion.24
  71.6 0.0 copy-done.3
  71.7 0.1 multiply_reduce_fusion
  71.8 0.1 sub.18
  71.8 1.5 %constant_dynamic-slice_fusion = bf16[64,512]{1,0:T(8,128)(2,1)} fusion(bf16[64,1024]{1,0:T(8,128)(2,1)} %add_convert_fusion, s32[]{:T(128)S(6)} %select_n.39), kind=kLoop, calls=%fused_computation.52 | loop fusion | bytes 131076 | tf_op jit(solution)/shard_map/dynamic_slice | solution.py:69
  73.3 20.5 %all-gather.2.cloned.1.call-done = bf16[512,1024]{1,0:T(8,128)(2,1)} async-done(((bf16[64,1024]{1,0:T(8,128)(2,1)}), bf16[512,1024]{1,0:T(8,128)(2,1)}) %all-gather.2.cloned.1.call-update) | async-done | bytes 1048592 | tf_op jit(solution)/shard_map/all_gather | solution.py:71
  93.8 0.0 copy-done
  93.8 2.8 %select_reduce_fusion = (f32[512]{0:T(512)S(1)}, f32[512]{0:T(512)S(1)}) fusion(s32[512]{0:T(512)S(1)} %sub.18, bf16[512,1024]{1,0:T(8,128)(2,1)} %all-gather.2.cloned.1.call-done, bf16[1024,1024]{1,0:T(8,128)(2,1)S(1)} %copy-done), kind=kOutput, calls=%fused_computation.2 | convolution fusion | flops 1075837952 | bytes 3151872 | tf_op jit(solution)/shard_map/dot_general | solution.py:70
  96.6 7.4 %all-reduce = (f32[512]{0:T(512)S(1)}, f32[512]{0:T(512)S(1)}) all-reduce(f32[512]{0:T(512)S(1)} %get-tuple-element.3, f32[512]{0:T(512)S(1)} %get-tuple-element.2), channel_id=1, replica_groups=mesh['groups'=2,'item'=4,'dp'=2,'tensor'=2] {'dp','tensor'}, use_global_device_ids=true, to_apply=%region_10.11 | all-reduce | flops 1024 | bytes 8192 | tf_op jit(solution)/shard_map/psum | solution.py:11
  104.1 10.2 %all-reduce.1 = (f32[512]{0:T(512)S(1)}, f32[512]{0:T(512)S(1)}) all-reduce(f32[512]{0:T(512)S(1)} %get-tuple-element.4, f32[512]{0:T(512)S(1)} %get-tuple-element.5), channel_id=1, replica_groups=mesh['groups'=2,'item'=4,'dp'=2,'tensor'=2] {'item'}, use_global_device_ids=true, to_apply=%region_11.12 | all-reduce | flops 1024 | bytes 8192 | tf_op jit(solution)/shard_map/psum | solution.py:12
  114.3 0.6 log_subtract_fusion
  (7 shorter events, 0.1 us)
Async XLA Ops:
  7.2 86.7 %copy-start = (bf16[1024,1024]{1,0:T(8,128)(2,1)S(1)}, bf16[1024,1024]{1,0:T(8,128)(2,1)}, u32[]{:S(2)}) copy-start(bf16[1024,1024]{1,0:T(8,128)(2,1)} %param.15) | copy-start | bytes 6291460
  7.2 62.7 %all-reduce.4.cloned.1.call-start = ((), (), s32[]{:S(2)}) async-start(), calls=%async_computation | async-start | bytes 524288 | tf_op jit(solution)/shard_map/psum | solution.py:67
  10.3 28.6 %copy-start.5 = (s32[8]{0:T(128)S(1)}, s32[8]{0:T(128)}, u32[]{:S(2)}) copy-start(s32[8]{0:T(128)} %param.9) | copy-start | bytes 100
  35.0 5.2 %copy-start.1 = (bf16[1024,1,2,128]{3,2,0,1:T(2,128)(2,1)S(1)}, bf16[1024,1,2,128]{3,2,0,1:T(2,128)(2,1)}, u32[]{:S(2)}) copy-start(bf16[1024,1,2,128]{3,2,0,1:T(2,128)(2,1)} %slice.18) | copy-start | bytes 1572868
  40.2 2.6 %copy-start.2 = (bf16[128,1024]{1,0:T(8,128)(2,1)S(1)}, bf16[128,1024]{1,0:T(8,128)(2,1)}, u32[]{:S(2)}) copy-start(bf16[128,1024]{1,0:T(8,128)(2,1)} %param.14) | copy-start | bytes 786436
  42.4 29.2 %copy-start.4 = (s32[8]{0:T(128)S(1)}, s32[8]{0:T(128)}, u32[]{:S(2)}) copy-start(s32[8]{0:T(128)} %param.10) | copy-start | bytes 100
  42.4 29.3 %copy-start.3 = (s32[8,64]{1,0:T(8,128)S(1)}, s32[8,64]{1,0:T(8,128)}, u32[]{:S(2)}) copy-start(s32[8,64]{1,0:T(8,128)} %param.12) | copy-start | bytes 6148
  43.8 50.0 %all-gather.2.cloned.1.call-start = ((), (), s32[]{:S(2)}) async-start(), calls=%async_computation.1 | async-start | bytes 1179648 | tf_op jit(solution)/shard_map/all_gather | solution.py:71
Sparse Core Ops, SparseCore 0:
  43.9 25.8 all-reduce.3
  71.7 22.0 all-gather.1
